TPU v7x, 32 devices: a whole 2x2x4 slice. The times are simulated.
32 devices in a mesh: ctx: 4 (over z), head: 4 (over y, x), fsdp: 2 (over core).
Axes of the slice: x: 2, y: 2, z: 4, core: 2. Of those that a mesh axis runs over, the one named last changes fastest.
Arguments:
- query_rows: bfloat16 [4096, 6144], P(('ctx', 'head'), 'fsdp'), may hold values from -400 to 400
- key_rows: bfloat16 [4096, 6144], P(('ctx', 'head'), 'fsdp'), may hold values from -8 to 8
- value_rows: bfloat16 [4096, 4096], P(('ctx', 'head'), 'fsdp'), may hold values from -6 to 6
- query_weight: bfloat16 [1536, 6144], P(('ctx', 'fsdp'), 'head'), may hold values from -6 to 6
- key_weight: bfloat16 [512, 4096], P(('ctx', 'fsdp'), 'head'), may hold values from -6 to 6
Outputs:
- attended: bfloat16 [4096, 4096], P('ctx', ('fsdp', 'head'))
- clipped_query: bfloat16 [1536, 6144], P(('ctx', 'fsdp'), 'head')
- clipped_key: bfloat16 [512, 4096], P(('ctx', 'fsdp'), 'head')
All inputs are finite; a program needn't handle non-finite values.
Results may differ from a plain program's by a relative error of at most 0.0033.
Values may be sent and summed in bfloat16 or wider, within the bound.
No kernel may reach another device: no remote copies, remote signals or barrier semaphores. Data moves between devices by JAX's collectives and lax.ppermute only.
A program may use at most 128 MiB of HBM per device.

v0:
```python
import jax
import jax.numpy as jnp
from jax import lax
from jax.sharding import PartitionSpec as P

DNOPE = 128
DROPE = 64
DV = 128
DQK = 192
clip_threshold = 100.0


def shifted_2(value, axis, steps):
    count = lax.axis_size(axis)
    first, last = (max(0, -steps), min(count, count - steps))
    return lax.ppermute(value, axis, [(source, source + steps) for source in range(first, last)])


def partial_softmax(scores, value_cube):
    highest = jnp.max(scores, axis=2)
    present = jnp.isfinite(highest)
    shifted = jnp.where(present, highest, 0.0)
    weights = jnp.exp(scores - shifted[:, :, None])
    totals = jnp.sum(weights, axis=2)
    rounded = weights.astype(jnp.bfloat16)
    summed = jnp.einsum("htu,uhd->thd", rounded, value_cube, preferred_element_type=jnp.float32)
    return (summed, totals, jnp.where(present, highest, -jnp.inf))


def merge_parts(own_part, far_part):
    own_sum, own_total, own_high = own_part
    far_sum, far_total, far_high = far_part
    highest = jnp.maximum(own_high, far_high)
    own_scale = jnp.exp(own_high - highest)
    far_scale = jnp.exp(far_high - highest)
    totals = own_total * own_scale + far_total * far_scale
    mixed = own_sum * own_scale.T[:, :, None] + far_sum * far_scale.T[:, :, None]
    return mixed / totals.T[:, :, None]


def head_scores(query_cube, key_cube):
    return jnp.einsum(
        "thd,uhd->htu", query_cube, key_cube, preferred_element_type=jnp.float32
    ) * DQK ** (-0.5)


def causal_block(query_cube, key_cube, value_cube, row_start, block_rows):
    row_count = key_cube.shape[0]
    query_block = query_cube[row_start : row_start + block_rows]
    row_ids = lax.broadcasted_iota(jnp.int32, (block_rows, row_count), 0) + row_start
    col_ids = lax.broadcasted_iota(jnp.int32, (block_rows, row_count), 1)
    scores = jnp.where((row_ids >= col_ids)[None], head_scores(query_block, key_cube), -jnp.inf)
    return (partial_softmax(scores, value_cube), jnp.max(scores, axis=(1, 2)))


def body(query_rows, key_rows, value_rows, query_weight, key_weight):
    local_query, local_key, local_value = (
        lax.all_to_all(query_rows, "head", split_axis=1, concat_axis=0, tiled=True),
        lax.all_to_all(key_rows, "head", split_axis=1, concat_axis=0, tiled=True),
        lax.all_to_all(value_rows, "head", split_axis=1, concat_axis=0, tiled=True),
    )
    row_count = local_query.shape[0]
    head_count = local_query.shape[1] // DQK
    query_cube = local_query.reshape(row_count, head_count, DQK)
    key_cube = local_key.reshape(row_count, head_count, DQK)
    value_cube = local_value.reshape(row_count, head_count, DV)
    block_index = lax.axis_index("ctx")
    block_rows = min(512, row_count)
    row_starts = list(range(0, row_count, block_rows))
    local_peak = jnp.full((head_count,), -jnp.inf, jnp.float32)
    pieces = []
    far_key, far_value = shifted_2((local_key, local_value), "ctx", 1)
    far_keys = far_key.reshape(row_count, head_count, DQK)
    far_values = far_value.reshape(row_count, head_count, DV)
    for row_start in row_starts:
        own_part, own_peak = causal_block(query_cube, key_cube, value_cube, row_start, block_rows)
        far_scores = jnp.where(
            block_index > 0,
            head_scores(query_cube[row_start : row_start + block_rows], far_keys),
            -jnp.inf,
        )
        far_part = partial_softmax(far_scores, far_values)
        local_peak = jnp.maximum(
            local_peak, jnp.maximum(own_peak, jnp.max(far_scores, axis=(1, 2)))
        )
        pieces.append(merge_parts(own_part, far_part))
    attended = (
        jnp.concatenate(pieces, axis=0).astype(jnp.bfloat16).reshape(row_count, head_count * DV)
    )
    weight_heads = key_weight.shape[1] // DNOPE
    cycle_peak = lax.pmax(local_peak, "ctx")
    gathered = lax.all_gather(cycle_peak, ("head", "fsdp"), axis=0, tiled=True)
    head_peak = (
        gathered.reshape(lax.axis_size("head"), lax.axis_size("fsdp"), head_count)
        .transpose(1, 0, 2)
        .reshape(-1)
    )
    own_peaks = lax.dynamic_slice_in_dim(
        head_peak, lax.axis_index("head") * weight_heads, weight_heads, 0
    )
    factor = jnp.minimum(1.0, clip_threshold / own_peaks)
    root_factor = jnp.sqrt(factor)
    column_factor = jnp.concatenate(
        [
            jnp.broadcast_to(root_factor[:, None], (weight_heads, DNOPE)),
            jnp.broadcast_to(factor[:, None], (weight_heads, DROPE)),
        ],
        axis=1,
    )
    query_count = query_weight.shape[0]
    key_count = key_weight.shape[0]
    clipped_query = (
        (
            query_weight.astype(jnp.float32).reshape(query_count, weight_heads, DQK)
            * column_factor[None]
        )
        .astype(jnp.bfloat16)
        .reshape(query_count, weight_heads * DQK)
    )
    clipped_key = (
        (
            key_weight.astype(jnp.float32).reshape(key_count, weight_heads, DNOPE)
            * root_factor[None, :, None]
        )
        .astype(jnp.bfloat16)
        .reshape(key_count, weight_heads * DNOPE)
    )
    return (attended, clipped_query, clipped_key)


def solution(mesh):
    return jax.shard_map(
        body,
        mesh=mesh,
        in_specs=(
            P(("ctx", "head"), "fsdp"),
            P(("ctx", "head"), "fsdp"),
            P(("ctx", "head"), "fsdp"),
            P(("ctx", "fsdp"), "head"),
            P(("ctx", "fsdp"), "head"),
        ),
        out_specs=(
            P("ctx", ("fsdp", "head")),
            P(("ctx", "fsdp"), "head"),
            P(("ctx", "fsdp"), "head"),
        ),
        check_vma=False,
    )
```

profile of v0, /device:TPU:0, one launch (start us, length us, event | category | flops | bytes accessed | tf_op | source)
XLA Modules:
  0.0 180.5 jit_solution(10534738147140960069)
XLA Ops:
  0.6 0.0 copy-start.13
  0.6 2.3 %copy.29 = bf16[256,2048]{0,1:T(8,128)(2,1)} copy(bf16[256,2048]{1,0:T(8,128)(2,1)} %param.7) | data formatting | bytes 2097152 | tf_op args[2]
  2.9 5.2 %all-to-all-start.2 = ((bf16[256,4,512]{0,2,1:T(8,128)(2,1)}), bf16[256,4,512]{0,2,1:T(8,128)(2,1)S(1)}, u32[]{:S(2)}, u32[]{:S(2)}) async-start(bf16[256,4,512]{0,2,1:T(8,128)(2,1)} %bitcast.5), calls=%async_computation.2 | async-start | bytes 2097152 | tf_op jit(solution)/shard_map/all_to_all | solution.py:60
  8.1 2.6 %copy.26 = bf16[256,3072]{0,1:T(8,128)(2,1)} copy(bf16[256,3072]{1,0:T(8,128)(2,1)} %param.6) | data formatting | bytes 3145728 | tf_op args[1]
  10.7 11.0 %all-to-all-done.2 = bf16[256,4,512]{0,2,1:T(8,128)(2,1)S(1)} async-done(((bf16[256,4,512]{0,2,1:T(8,128)(2,1)}), bf16[256,4,512]{0,2,1:T(8,128)(2,1)S(1)}, u32[]{:S(2)}, u32[]{:S(2)}) %all-to-all-start.2) | async-done | bytes 1048608 | tf_op jit(solution)/shard_map/all_to_all | solution.py:60
  21.7 3.6 %all-to-all-start.1 = ((bf16[256,4,768]{0,2,1:T(8,128)(2,1)}), bf16[256,4,768]{0,2,1:T(8,128)(2,1)S(1)}, u32[]{:S(2)}, u32[]{:S(2)}) async-start(bf16[256,4,768]{0,2,1:T(8,128)(2,1)} %bitcast.115), calls=%async_computation.1 | async-start | bytes 3145728 | tf_op jit(solution)/shard_map/all_to_all | solution.py:59
  25.3 2.6 %copy.24 = bf16[256,3072]{0,1:T(8,128)(2,1)} copy(bf16[256,3072]{1,0:T(8,128)(2,1)} %param.5) | data formatting | bytes 3145728 | tf_op args[0]
  27.9 16.1 %all-to-all-done.1 = bf16[256,4,768]{0,2,1:T(8,128)(2,1)S(1)} async-done(((bf16[256,4,768]{0,2,1:T(8,128)(2,1)}), bf16[256,4,768]{0,2,1:T(8,128)(2,1)S(1)}, u32[]{:S(2)}, u32[]{:S(2)}) %all-to-all-start.1) | async-done | bytes 1572896 | tf_op jit(solution)/shard_map/all_to_all | solution.py:59
  44.0 4.3 %all-to-all-start = ((bf16[256,4,768]{0,2,1:T(8,128)(2,1)}), bf16[256,4,768]{0,2,1:T(8,128)(2,1)}, u32[]{:S(2)}, u32[]{:S(2)}) async-start(bf16[256,4,768]{0,2,1:T(8,128)(2,1)} %bitcast.114), calls=%async_computation | async-start | bytes 3145728 | tf_op jit(solution)/shard_map/all_to_all | solution.py:58
  48.4 0.0 copy-done.13
  48.4 0.6 dynamic-slice
  49.7 1.0 iota_compare_fusion.1
  50.6 1.2 iota_compare_fusion
  51.8 1.8 copy.31
  53.6 2.6 %reshape.100 = bf16[1024,4,128]{0,2,1:T(8,128)(2,1)} reshape(bf16[4,256,512]{1,0,2:T(4,128)(2,1)} %copy.31) | data formatting | bytes 2097152 | tf_op jit(solution)/shard_map/reshape | solution.py:66
  56.1 1.3 copy.30
  57.4 4.5 %collective-permute-start.1 = (bf16[1024,512]{1,0:T(8,128)(2,1)}, bf16[1024,512]{1,0:T(8,128)(2,1)}, u32[]{:S(2)}, u32[]{:S(2)}) collective-permute-start(bf16[1024,512]{1,0:T(8,128)(2,1)} %bitcast.118), channel_id=1, source_target_pairs={{0,8},{8,16},{16,24},{1,9},{9,17},{17,25},{2,10},{10,18},{18,26},{... | collective-permute-start | bytes 3145736 | tf_op jit(solution)/shard_map/ppermute | solution.py:16
  62.0 1.6 copy.27
  63.6 3.6 %collective-permute-start = (bf16[1024,768]{1,0:T(8,128)(2,1)}, bf16[1024,768]{1,0:T(8,128)(2,1)}, u32[]{:S(2)}, u32[]{:S(2)}) collective-permute-start(bf16[1024,768]{1,0:T(8,128)(2,1)} %bitcast.10), channel_id=1, source_target_pairs={{0,8},{8,16},{16,24},{1,9},{9,17},{17,25},{2,10},{10,18},{18,26},{... | collective-permute-start | bytes 4718600 | tf_op jit(solution)/shard_map/ppermute | solution.py:16
  67.2 0.0 all-to-all-done
  67.2 1.5 fusion.81
  68.7 0.8 copy.34
  69.5 1.4 slice.17
  70.9 0.8 copy.25
  71.7 1.4 slice.15
  73.1 1.2 copy.28
  74.3 0.0 copy-start.5
  74.3 2.5 %reshape.99 = bf16[1024,4,192]{0,2,1:T(8,128)(2,1)} reshape(bf16[4,256,768]{1,0,2:T(4,128)(2,1)S(1)} %copy.28) | data formatting | bytes 3145728 | tf_op jit(solution)/shard_map/reshape | solution.py:65
  76.8 3.8 %fusion.13 = (f32[4,512]{1,0:T(4,128)S(1)}, f32[4,512,1024]{2,1,0:T(8,128)S(1)}) fusion(pred[512,1024]{1,0:T(8,128)(4,1)} %iota_compare_fusion, bf16[512,4,192]{0,2,1:T(8,128)(2,1)} %slice.17, bf16[1024,4,192]{0,2,1:T(8,128)(2,1)} %reshape.99), kind=kOutput, calls=%fused_computation.21 | convolution fusion | flops 811595776 | bytes 11280384 | tf_op jit(solution)/shard_map/thd,uhd->htu/dot_general | solution.py:42
  80.6 0.0 copy-done.5
  80.7 0.0 copy-start.4
  80.7 1.9 %fusion.9 = (f32[4,512]{1,0:T(4,128)S(1)}, f32[4,512,1024]{2,1,0:T(8,128)S(1)}) fusion(pred[512,1024]{1,0:T(8,128)(4,1)S(1)} %copy-done.5, bf16[512,4,192]{0,2,1:T(8,128)(2,1)S(1)} %copy-done.9, bf16[1024,4,192]{0,2,1:T(8,128)(2,1)S(1)} %copy-done.6), kind=kOutput, calls=%fused_computation.17 | convolution fusion | flops 811595776 | bytes 11280384 | tf_op jit(solution)/shard_map/thd,uhd->htu/dot_general | solution.py:42
  82.7 5.6 %fusion.8 = (f32[4]{0:T(128)S(1)}, f32[4,512]{1,0:T(4,128)S(1)}, f32[4,512]{1,0:T(4,128)S(1)}, f32[4]{0:T(128)S(1)}) fusion(f32[4,512,1024]{2,1,0:T(8,128)S(1)} %get-tuple-element.26, pred[512,1024]{1,0:T(8,128)(4,1)S(1)} %copy-done.5, f32[4,512]{1,0:T(4,128)S(1)} %is-finite_select_fusion.7, f32[4,512]{1,0:T(4,128)S(1)} %is-finite_select_fusion.3, ...), kind=kLoop, calls=%fused_computation.16 | loop fusion | flops 20967416 | bytes 17858592 | tf_op jit(solution)/shard_map/reduce_max | solution.py:53
  88.3 0.0 copy-done.3
  88.3 28.4 %collective-permute-done = bf16[1024,768]{1,0:T(8,128)(2,1)} collective-permute-done((bf16[1024,768]{1,0:T(8,128)(2,1)}, bf16[1024,768]{1,0:T(8,128)(2,1)}, u32[]{:S(2)}, u32[]{:S(2)}) %collective-permute-start) | collective-permute-done | bytes 1572896 | tf_op jit(solution)/shard_map/ppermute | solution.py:16
  116.6 1.7 copy.32
  118.4 1.5 fusion.15
  119.9 0.0 copy-done.10
  119.9 0.0 copy-start
  119.9 1.5 fusion.11
  121.5 4.6 %fusion.10 = (f32[4]{0:T(128)S(1)}, f32[4,512]{1,0:T(4,128)S(1)}, f32[4,512]{1,0:T(4,128)S(1)}, f32[4]{0:T(128)S(1)}) fusion(f32[4,512,1024]{2,1,0:T(8,128)S(1)} %get-tuple-element.28, pred[]{:T(512)S(6)} %gt.4, f32[4,512]{1,0:T(4,128)S(1)} %is-finite_select_fusion.4, f32[4,512]{1,0:T(4,128)S(1)} %is-finite_select_fusion, ...), kind=kLoop, calls=%fused_computation.18 | loop fusion | flops 20967416 | bytes 16810016 | tf_op jit(solution)/shard_map/reduce_max | solution.py:84
  126.0 0.0 collective-permute-done.1
  126.1 1.5 copy.33
  127.6 12.9 %pmax.7 = f32[4]{0:T(128)S(1)} all-reduce(f32[4]{0:T(128)S(1)} %maximum_maximum_fusion), channel_id=1, replica_groups=mesh['ctx'=4,'head'=4,'fsdp'=2] {'ctx'}, use_global_device_ids=true, to_apply=%region_12.13 | all-reduce | flops 4 | bytes 32 | tf_op jit(solution)/shard_map/pmax | solution.py:91
  140.4 0.2 dynamic-update-slice
  140.7 0.1 reshape.103
  140.8 0.1 reshape.104
  140.8 12.0 %all-reduce.1 = f32[32]{0:T(128)S(1)} all-reduce(f32[32]{0:T(128)S(1)} %reshape.104), channel_id=1, replica_groups=mesh['ctx'=4,'head'=4,'fsdp'=2] {'head','fsdp'}, use_global_device_ids=true, to_apply=%add | all-reduce | flops 32 | bytes 256
  152.9 0.1 fusion.76
  152.9 0.1 broadcast_bitcast_fusion
  153.0 0.1 broadcast_in_dim.65
  153.1 0.1 broadcast_in_dim.66
  153.2 0.1 mul.102
  153.3 4.7 %fusion.49 = f32[512,4,128]{0,2,1:T(8,128)S(1)} fusion(bf16[1024,4,128]{0,2,1:T(8,128)(2,1)S(1)} %copy-done.7, f32[4,512,1024]{2,1,0:T(8,128)} %copy-done.3, f32[4,512]{1,0:T(4,128)S(1)} %is-finite_select_fusion.7, pred[512,1024]{1,0:T(8,128)(4,1)S(1)} %copy-done.5, f32[512,4]{0,1:T(4,128)S(1)} %get-tuple-element.15), kind=kOutput, calls=%fused_computation.41 | convolution fusion | flops 545521664 | bytes 11026432 | tf_op jit(solution)/shard_map/htu,uhd->thd/dot_general | solution.py:26
  158.0 6.3 %divide_convert_fusion.1 = bf16[512,4,128]{0,2,1:T(8,128)(2,1)} fusion(f32[512,4,128]{0,2,1:T(8,128)S(1)} %fusion.49, bf16[1024,4,128]{0,2,1:T(8,128)(2,1)S(1)} %bitcast.119, f32[4,512,1024]{2,1,0:T(8,128)} %copy-done.1, f32[4,512]{1,0:T(4,128)S(1)} %is-finite_select_fusion.4, pred[]{:T(512)S(6)} %gt.4, f32[512,4]{0,1:T(4,128)S(1)} %get-tuple-element.13, ...), kind=kOutput, calls=%fused_computation.47 | convolution fusion | flops 546308096 | bytes 11034625 | tf_op jit(solution)/shard_map/htu,uhd->thd/dot_general | solution.py:26
  164.2 1.3 copy.35
  165.5 4.7 %fusion.46 = f32[512,4,128]{0,2,1:T(8,128)S(1)} fusion(bf16[1024,4,128]{0,2,1:T(8,128)(2,1)S(1)} %copy-done.7, f32[4,512,1024]{2,1,0:T(8,128)} %copy-done.2, f32[4,512]{1,0:T(4,128)S(1)} %is-finite_select_fusion.3, pred[512,1024]{1,0:T(8,128)(4,1)S(1)} %copy-done.4, f32[512,4]{0,1:T(4,128)S(1)} %get-tuple-element.18), kind=kOutput, calls=%fused_computation.40 | convolution fusion | flops 545521664 | bytes 11026432 | tf_op jit(solution)/shard_map/htu,uhd->thd/dot_general | solution.py:26
  170.2 0.0 copy-start.11
  170.2 0.0 copy-start.12
  170.2 6.3 %divide_convert_fusion = bf16[512,4,128]{0,2,1:T(8,128)(2,1)} fusion(f32[512,4,128]{0,2,1:T(8,128)S(1)} %fusion.46, bf16[1024,4,128]{0,2,1:T(8,128)(2,1)S(1)} %bitcast.120, f32[4,512,1024]{2,1,0:T(8,128)} %copy-done, f32[4,512]{1,0:T(4,128)S(1)} %is-finite_select_fusion, pred[]{:T(512)S(6)} %gt.4, f32[512,4]{0,1:T(4,128)S(1)} %get-tuple-element.16, ...), kind=kOutput, calls=%fused_computation.46 | convolution fusion | flops 546308096 | bytes 11034625 | tf_op jit(solution)/shard_map/htu,uhd->thd/dot_general | solution.py:26
  176.6 1.3 copy.36
  177.8 0.9 multiply_convert_fusion
  178.7 0.7 multiply_convert_fusion.1
  179.4 1.0 pad_maximum_fusion
  (29 shorter events, 0.1 us)
Async XLA Ops:
  0.6 47.8 %copy-start.13 = (u32[32]{0:T(128)S(1)}, u32[32]{0:T(128)}, u32[]{:S(2)}) copy-start(u32[32]{0:T(128)} %constant.30) | copy-start | bytes 388
  2.9 18.8 %all-to-all-start.2 = ((bf16[256,4,512]{0,2,1:T(8,128)(2,1)}), bf16[256,4,512]{0,2,1:T(8,128)(2,1)S(1)}, u32[]{:S(2)}, u32[]{:S(2)}) async-start(bf16[256,4,512]{0,2,1:T(8,128)(2,1)} %bitcast.5), calls=%async_computation.2 | async-start | bytes 2097152 | tf_op jit(solution)/shard_map/all_to_all | solution.py:60
  21.7 22.3 %all-to-all-start.1 = ((bf16[256,4,768]{0,2,1:T(8,128)(2,1)}), bf16[256,4,768]{0,2,1:T(8,128)(2,1)S(1)}, u32[]{:S(2)}, u32[]{:S(2)}) async-start(bf16[256,4,768]{0,2,1:T(8,128)(2,1)} %bitcast.115), calls=%async_computation.1 | async-start | bytes 3145728 | tf_op jit(solution)/shard_map/all_to_all | solution.py:59
  44.0 23.2 %all-to-all-start = ((bf16[256,4,768]{0,2,1:T(8,128)(2,1)}), bf16[256,4,768]{0,2,1:T(8,128)(2,1)}, u32[]{:S(2)}, u32[]{:S(2)}) async-start(bf16[256,4,768]{0,2,1:T(8,128)(2,1)} %bitcast.114), calls=%async_computation | async-start | bytes 3145728 | tf_op jit(solution)/shard_map/all_to_all | solution.py:58
  57.4 68.6 %collective-permute-start.1 = (bf16[1024,512]{1,0:T(8,128)(2,1)}, bf16[1024,512]{1,0:T(8,128)(2,1)}, u32[]{:S(2)}, u32[]{:S(2)}) collective-permute-start(bf16[1024,512]{1,0:T(8,128)(2,1)} %bitcast.118), channel_id=1, source_target_pairs={{0,8},{8,16},{16,24},{1,9},{9,17},{17,25},{2,10},{10,18},{18,26},{... | collective-permute-start | bytes 3145736 | tf_op jit(solution)/shard_map/ppermute | solution.py:16
  63.6 53.1 %collective-permute-start = (bf16[1024,768]{1,0:T(8,128)(2,1)}, bf16[1024,768]{1,0:T(8,128)(2,1)}, u32[]{:S(2)}, u32[]{:S(2)}) collective-permute-start(bf16[1024,768]{1,0:T(8,128)(2,1)} %bitcast.10), channel_id=1, source_target_pairs={{0,8},{8,16},{16,24},{1,9},{9,17},{17,25},{2,10},{10,18},{18,26},{... | collective-permute-start | bytes 4718600 | tf_op jit(solution)/shard_map/ppermute | solution.py:16
  74.3 6.3 %copy-start.5 = (pred[512,1024]{1,0:T(8,128)(4,1)S(1)}, pred[512,1024]{1,0:T(8,128)(4,1)}, u32[]{:S(2)}) copy-start(pred[512,1024]{1,0:T(8,128)(4,1)} %iota_compare_fusion.1) | copy-start | bytes 1572868
  76.8 3.8 %copy-start.6 = (bf16[1024,4,192]{0,2,1:T(8,128)(2,1)S(1)}, bf16[1024,4,192]{0,2,1:T(8,128)(2,1)}, u32[]{:S(2)}) copy-start(bf16[1024,4,192]{0,2,1:T(8,128)(2,1)} %reshape.99) | copy-start | bytes 4718596
  76.8 3.8 %copy-start.9 = (bf16[512,4,192]{0,2,1:T(8,128)(2,1)S(1)}, bf16[512,4,192]{0,2,1:T(8,128)(2,1)}, u32[]{:S(2)}) copy-start(bf16[512,4,192]{0,2,1:T(8,128)(2,1)} %slice.15) | copy-start | bytes 2359300
  80.7 7.6 %copy-start.2 = (f32[4,512,1024]{2,1,0:T(8,128)}, f32[4,512,1024]{2,1,0:T(8,128)S(1)}, u32[]{:S(2)}) copy-start(f32[4,512,1024]{2,1,0:T(8,128)S(1)} %get-tuple-element.22) | copy-start | bytes 25165828
  80.7 2.0 %copy-start.4 = (pred[512,1024]{1,0:T(8,128)(4,1)S(1)}, pred[512,1024]{1,0:T(8,128)(4,1)}, u32[]{:S(2)}) copy-start(pred[512,1024]{1,0:T(8,128)(4,1)} %iota_compare_fusion) | copy-start | bytes 1572868
  82.6 5.7 %copy-start.3 = (f32[4,512,1024]{2,1,0:T(8,128)}, f32[4,512,1024]{2,1,0:T(8,128)S(1)}, u32[]{:S(2)}) copy-start(f32[4,512,1024]{2,1,0:T(8,128)S(1)} %get-tuple-element.26) | copy-start | bytes 25165828
  82.6 35.7 %copy-start.8 = (bf16[512,4,192]{0,2,1:T(8,128)(2,1)S(1)}, bf16[512,4,192]{0,2,1:T(8,128)(2,1)}, u32[]{:S(2)}) copy-start(bf16[512,4,192]{0,2,1:T(8,128)(2,1)} %slice.17) | copy-start | bytes 2359300
  118.3 1.5 copy-start.10
  119.9 6.1 %copy-start = (f32[4,512,1024]{2,1,0:T(8,128)}, f32[4,512,1024]{2,1,0:T(8,128)S(1)}, u32[]{:S(2)}) copy-start(f32[4,512,1024]{2,1,0:T(8,128)S(1)} %get-tuple-element.24) | copy-start | bytes 25165828
  121.4 4.6 %copy-start.1 = (f32[4,512,1024]{2,1,0:T(8,128)}, f32[4,512,1024]{2,1,0:T(8,128)S(1)}, u32[]{:S(2)}) copy-start(f32[4,512,1024]{2,1,0:T(8,128)S(1)} %get-tuple-element.28) | copy-start | bytes 25165828
  121.5 31.8 %copy-start.7 = (bf16[1024,4,128]{0,2,1:T(8,128)(2,1)S(1)}, bf16[1024,4,128]{0,2,1:T(8,128)(2,1)}, u32[]{:S(2)}) copy-start(bf16[1024,4,128]{0,2,1:T(8,128)(2,1)} %reshape.100) | copy-start | bytes 3145732
  170.2 7.6 %copy-start.11 = (bf16[192,1536]{1,0:T(8,128)(2,1)S(1)}, bf16[192,1536]{1,0:T(8,128)(2,1)}, u32[]{:S(2)}) copy-start(bf16[192,1536]{1,0:T(8,128)(2,1)} %param.8) | copy-start | bytes 1769476
  170.2 8.5 %copy-start.12 = (bf16[64,1024]{1,0:T(8,128)(2,1)S(1)}, bf16[64,1024]{1,0:T(8,128)(2,1)}, u32[]{:S(2)}) copy-start(bf16[64,1024]{1,0:T(8,128)(2,1)} %param.9) | copy-start | bytes 393220
where the time goes:
time: 181 us; the launch traced here: 180 us
  waiting for transfers between devices  55.5 us (31%)
  local copies, waits for them, and re-layouts  31.4 us (17%)
  matrix products  30.7 us (17%)
  blocking collectives  24.9 us (14%)
  starting transfers between devices  21.2 us (12%)
  other arithmetic  15.1 us (8%)
    ppermute x2, waiting for transfers between devices, shifted_2(): lax.ppermute(value, axis, [(source, source + steps) for source in range(f...  28.4 us
    dot_general x4, matrix products, partial_softmax(): jnp.einsum('htu,uhd->thd', rounded, value_cube, preferred_element_type=jn...  22 us
    all_to_all x1, waiting for transfers between devices, body(): lax.all_to_all(key_rows, 'head', split_axis=1, concat_axis=0, tiled=True)  16.1 us
    pmax x1, blocking collectives, body(): cycle_peak = lax.pmax(local_peak, 'ctx')  12.9 us
    unnamed x1, blocking collectives  12 us
    all_to_all x1, waiting for transfers between devices, body(): lax.all_to_all(value_rows, 'head', split_axis=1, concat_axis=0, tiled=True)  11 us
    dot_general x4, matrix products, head_scores(): jnp.einsum('thd,uhd->htu', query_cube, key_cube, preferred_element_type=j...  8.76 us
    unnamed x34, local copies, waits for them, and re-layouts  8.34 us
  transfers between devices with their start and end apart: 5, of which 3 were waited for; matrix products, arithmetic and copies ran while one was open for 25% of the time, Pallas kernels for 0%

commit v1 on v0

--- a/solution.py
+++ b/solution.py
@@ -57,7 +57,12 @@
     local_query, local_key, local_value = (
         lax.all_to_all(query_rows, "head", split_axis=1, concat_axis=0, tiled=True),
         lax.all_to_all(key_rows, "head", split_axis=1, concat_axis=0, tiled=True),
-        lax.all_to_all(value_rows, "head", split_axis=1, concat_axis=0, tiled=True),
+        jnp.concatenate(
+            lax.all_to_all(
+                jnp.stack(jnp.split(value_rows, lax.axis_size("head"), axis=1)), "head", 0, 0
+            ),
+            axis=0,
+        ),
     )
     row_count = local_query.shape[0]
     head_count = local_query.shape[1] // DQK

time: 181 us -> 172 us (0.950)
  waiting for transfers between devices: 55.5 us -> 38.2 us
  blocking collectives: 24.9 us -> 38.2 us
  local copies, waits for them, and re-layouts: 31.4 us -> 26.9 us
  matrix products: 30.7 us -> 27.6 us
  starting transfers between devices: 21.2 us -> 23.2 us
    ppermute x2, waiting for transfers between devices: 28.4 us -> 6.63 us  [shifted_2(): lax.ppermute(value, axis, [(source, source + steps) for source in range(f...]
    pmax x1, blocking collectives: 12.9 us -> 26.2 us  [body(): cycle_peak = lax.pmax(local_peak, 'ctx')]
    another operation x0 -> x3, local copies, waits for them, and re-layouts: none -> 4.79 us  [the longest x2 3.53 us: body(): value_cube = local_value.reshape(row_count, head_count, DV)]
    all_to_all x1, waiting for transfers between devices: 0.01 us -> 4.35 us  [body(): lax.all_to_all(query_rows, 'head', split_axis=1, concat_axis=0, tiled=True)]
    dot_general x4, matrix products: 22 us -> 18.8 us  [partial_softmax(): jnp.einsum('htu,uhd->thd', rounded, value_cube, preferred_element_type=jn...]
    all_to_all x2 -> x0, local copies, waits for them, and re-layouts: 3.09 us -> none  [body(): lax.all_to_all(value_rows, 'head', split_axis=1, concat_axis=0, tiled=True)]
    concatenate x2, local copies, waits for them, and re-layouts: 2.5 us -> 0.43 us  [body(): jnp.concatenate(pieces, axis=0).astype(jnp.bfloat16)]
    ppermute x2, starting transfers between devices: 8.16 us -> 10.1 us  [shifted_2(): lax.ppermute(value, axis, [(source, source + steps) for source in range(f...]
  transfers between devices with their start and end apart: 5 -> 5, of which waited for: 3 -> 4; matrix products, arithmetic and copies ran while one was open for 25% -> 24% of each run, Pallas kernels for 0% -> 0%
where the time goes in v1:
time: 172 us
  waiting for transfers between devices  38.2 us (22%)
  blocking collectives  38.2 us (22%)
  matrix products  27.6 us (16%)
  local copies, waits for them, and re-layouts  26.9 us (16%)
  starting transfers between devices  23.2 us (13%)
  other arithmetic  16.2 us (9%)
    pmax x1, blocking collectives, body(): cycle_peak = lax.pmax(local_peak, 'ctx')  26.2 us
    dot_general x4, matrix products, partial_softmax(): jnp.einsum('htu,uhd->thd', rounded, value_cube, preferred_element_type=jn...  18.8 us
    all_to_all x1, waiting for transfers between devices, body(): lax.all_to_all(key_rows, 'head', split_axis=1, concat_axis=0, tiled=True)  16.1 us
    unnamed x1, blocking collectives  12 us
    all_to_all x1, waiting for transfers between devices, body(): lax.all_to_all(jnp.stack(jnp.split(value_rows, lax.axis_size('head'), axi...  11 us
    ppermute x2, starting transfers between devices, shifted_2(): lax.ppermute(value, axis, [(source, source + steps) for source in range(f...  10.1 us
    dot_general x4, matrix products, head_scores(): jnp.einsum('thd,uhd->htu', query_cube, key_cube, preferred_element_type=j...  8.76 us
    unnamed x37, local copies, waits for them, and re-layouts  7.07 us
  transfers between devices with their start and end apart: 5, of which 4 were waited for; matrix products, arithmetic and copies ran while one was open for 24% of the time, Pallas kernels for 0%

profile of v1, /device:TPU:0, one launch (start us, length us, event | category | flops | bytes accessed | tf_op | source)
XLA Modules:
  0.0 171.8 jit_solution(17447646202404038495)
XLA Ops:
  0.6 1.3 slice_bitcast_fusion.3
  1.9 0.0 copy-start.15
  1.9 1.1 pad_maximum_fusion
  3.0 5.2 %all-to-all-start = ((bf16[4,256,512]{2,1,0:T(8,128)(2,1)}), bf16[4,256,512]{2,1,0:T(8,128)(2,1)S(1)}, u32[]{:S(2)}, u32[]{:S(2)}) async-start(bf16[4,256,512]{2,1,0:T(8,128)(2,1)} %pad_maximum_fusion), calls=%async_computation | async-start | bytes 2097152 | tf_op jit(solution)/shard_map/all_to_all | solution.py:61
  8.2 2.6 %copy.28 = bf16[256,3072]{0,1:T(8,128)(2,1)} copy(bf16[256,3072]{1,0:T(8,128)(2,1)} %param.6) | data formatting | bytes 3145728 | tf_op args[1]
  10.8 11.0 %all-to-all-done = bf16[4,256,512]{2,1,0:T(8,128)(2,1)S(1)} async-done(((bf16[4,256,512]{2,1,0:T(8,128)(2,1)}), bf16[4,256,512]{2,1,0:T(8,128)(2,1)S(1)}, u32[]{:S(2)}, u32[]{:S(2)}) %all-to-all-start) | async-done | bytes 1048608 | tf_op jit(solution)/shard_map/all_to_all | solution.py:61
  21.8 3.6 %all-to-all-start.2 = ((bf16[256,4,768]{0,2,1:T(8,128)(2,1)}), bf16[256,4,768]{0,2,1:T(8,128)(2,1)S(1)}, u32[]{:S(2)}, u32[]{:S(2)}) async-start(bf16[256,4,768]{0,2,1:T(8,128)(2,1)} %bitcast.117), calls=%async_computation.2 | async-start | bytes 3145728 | tf_op jit(solution)/shard_map/all_to_all | solution.py:59
  25.4 2.6 %copy.26 = bf16[256,3072]{0,1:T(8,128)(2,1)} copy(bf16[256,3072]{1,0:T(8,128)(2,1)} %param.5) | data formatting | bytes 3145728 | tf_op args[0]
  28.0 16.1 %all-to-all-done.2 = bf16[256,4,768]{0,2,1:T(8,128)(2,1)S(1)} async-done(((bf16[256,4,768]{0,2,1:T(8,128)(2,1)}), bf16[256,4,768]{0,2,1:T(8,128)(2,1)S(1)}, u32[]{:S(2)}, u32[]{:S(2)}) %all-to-all-start.2) | async-done | bytes 1572896 | tf_op jit(solution)/shard_map/all_to_all | solution.py:59
  44.1 4.3 %all-to-all-start.1 = ((bf16[256,4,768]{0,2,1:T(8,128)(2,1)}), bf16[256,4,768]{0,2,1:T(8,128)(2,1)}, u32[]{:S(2)}, u32[]{:S(2)}) async-start(bf16[256,4,768]{0,2,1:T(8,128)(2,1)} %bitcast.116), calls=%async_computation.1 | async-start | bytes 3145728 | tf_op jit(solution)/shard_map/all_to_all | solution.py:58
  48.5 0.6 dynamic-slice
  49.8 1.0 iota_compare_fusion.1
  50.7 1.2 iota_compare_fusion
  51.9 1.1 reshape.106
  53.0 2.4 %copy.37 = bf16[1024,4,128]{0,2,1:T(8,128)(2,1)} copy(bf16[1024,4,128]{2,1,0:T(4,128)(2,1)} %reshape.106) | data formatting | bytes 2097152 | tf_op jit(solution)/shard_map/reshape;reshape | solution.py:71
  55.4 1.3 copy.32
  56.7 1.6 copy.29
  58.3 4.7 %collective-permute-start = (bf16[1024,768]{1,0:T(8,128)(2,1)}, bf16[1024,768]{1,0:T(8,128)(2,1)}, u32[]{:S(2)}, u32[]{:S(2)}) collective-permute-start(bf16[1024,768]{1,0:T(8,128)(2,1)} %bitcast.11), channel_id=1, source_target_pairs={{0,8},{8,16},{16,24},{1,9},{9,17},{17,25},{2,10},{10,18},{18,26},{... | collective-permute-start | bytes 4718600 | tf_op jit(solution)/shard_map/ppermute | solution.py:16
  63.0 4.3 %all-to-all-done.1 = bf16[256,4,768]{0,2,1:T(8,128)(2,1)} async-done(((bf16[256,4,768]{0,2,1:T(8,128)(2,1)}), bf16[256,4,768]{0,2,1:T(8,128)(2,1)}, u32[]{:S(2)}, u32[]{:S(2)}) %all-to-all-start.1) | async-done | bytes 1572896 | tf_op jit(solution)/shard_map/all_to_all | solution.py:58
  67.3 1.5 fusion.81
  68.8 0.8 copy.33
  69.6 1.4 slice.17
  71.0 0.8 copy.27
  71.8 1.4 slice.15
  73.2 1.2 copy.30
  74.4 2.5 %reshape.95 = bf16[1024,4,192]{0,2,1:T(8,128)(2,1)} reshape(bf16[4,256,768]{1,0,2:T(4,128)(2,1)S(1)} %copy.30) | data formatting | bytes 3145728 | tf_op jit(solution)/shard_map/reshape | solution.py:70
  76.9 3.8 %fusion.13 = (f32[4,512]{1,0:T(4,128)S(1)}, f32[4,512,1024]{2,1,0:T(8,128)S(1)}) fusion(pred[512,1024]{1,0:T(8,128)(4,1)} %iota_compare_fusion, bf16[512,4,192]{0,2,1:T(8,128)(2,1)} %slice.17, bf16[1024,4,192]{0,2,1:T(8,128)(2,1)} %reshape.95), kind=kOutput, calls=%fused_computation.21 | convolution fusion | flops 811595776 | bytes 11280384 | tf_op jit(solution)/shard_map/thd,uhd->htu/dot_general | solution.py:42
  80.7 0.0 copy-done.6
  80.8 0.0 copy-start.5
  80.8 1.9 %fusion.9 = (f32[4,512]{1,0:T(4,128)S(1)}, f32[4,512,1024]{2,1,0:T(8,128)S(1)}) fusion(pred[512,1024]{1,0:T(8,128)(4,1)S(1)} %copy-done.6, bf16[512,4,192]{0,2,1:T(8,128)(2,1)S(1)} %copy-done.11, bf16[1024,4,192]{0,2,1:T(8,128)(2,1)S(1)} %copy-done.7), kind=kOutput, calls=%fused_computation.17 | convolution fusion | flops 811595776 | bytes 11280384 | tf_op jit(solution)/shard_map/thd,uhd->htu/dot_general | solution.py:42
  82.8 5.6 %fusion.8 = (f32[4]{0:T(128)S(1)}, f32[4,512]{1,0:T(4,128)S(1)}, f32[4,512]{1,0:T(4,128)S(1)}, f32[4]{0:T(128)S(1)}) fusion(f32[4,512,1024]{2,1,0:T(8,128)S(1)} %get-tuple-element.30, pred[512,1024]{1,0:T(8,128)(4,1)S(1)} %copy-done.6, f32[4,512]{1,0:T(4,128)S(1)} %is-finite_select_fusion.7, f32[4,512]{1,0:T(4,128)S(1)} %is-finite_select_fusion.3, ...), kind=kLoop, calls=%fused_computation.16 | loop fusion | flops 20967416 | bytes 17858592 | tf_op jit(solution)/shard_map/reduce_max | solution.py:53
  88.4 0.0 copy-done.3
  88.4 0.0 copy-done.4
  88.4 6.6 %collective-permute-done = bf16[1024,768]{1,0:T(8,128)(2,1)} collective-permute-done((bf16[1024,768]{1,0:T(8,128)(2,1)}, bf16[1024,768]{1,0:T(8,128)(2,1)}, u32[]{:S(2)}, u32[]{:S(2)}) %collective-permute-start) | collective-permute-done | bytes 1572896 | tf_op jit(solution)/shard_map/ppermute | solution.py:16
  95.0 1.7 copy.31
  96.7 1.5 fusion.15
  98.3 1.5 fusion.11
  99.8 0.0 copy-start.9
  99.9 4.6 %fusion.10 = (f32[4]{0:T(128)S(1)}, f32[4,512]{1,0:T(4,128)S(1)}, f32[4,512]{1,0:T(4,128)S(1)}, f32[4]{0:T(128)S(1)}) fusion(f32[4,512,1024]{2,1,0:T(8,128)S(1)} %get-tuple-element.32, pred[]{:T(512)S(6)} %gt.4, f32[4,512]{1,0:T(4,128)S(1)} %is-finite_select_fusion.4, f32[4,512]{1,0:T(4,128)S(1)} %is-finite_select_fusion, ...), kind=kLoop, calls=%fused_computation.18 | loop fusion | flops 20967416 | bytes 16810016 | tf_op jit(solution)/shard_map/reduce_max | solution.py:89
  104.5 5.4 %collective-permute-start.1 = (bf16[1024,512]{0,1:T(8,128)(2,1)S(1)}, bf16[1024,512]{0,1:T(8,128)(2,1)}, u32[]{:S(2)}, u32[]{:S(2)}) collective-permute-start(bf16[1024,512]{0,1:T(8,128)(2,1)S(1)} %copy-done.9), channel_id=1, source_target_pairs={{0,8},{8,16},{16,24},{1,9},{9,17},{17,25},{2,10},{10,18},{18,26},{... | collective-permute-start | bytes 3145736 | tf_op jit(solution)/shard_map/ppermute | solution.py:16
  109.8 26.2 %pmax.7 = f32[4]{0:T(128)S(1)} all-reduce(f32[4]{0:T(128)S(1)} %maximum_maximum_fusion), channel_id=1, replica_groups=mesh['ctx'=4,'head'=4,'fsdp'=2] {'ctx'}, use_global_device_ids=true, to_apply=%region_12.13 | all-reduce | flops 4 | bytes 32 | tf_op jit(solution)/shard_map/pmax | solution.py:96
  136.0 0.2 dynamic-update-slice
  136.2 0.1 reshape.99
  136.3 0.1 reshape.100
  136.4 12.0 %all-reduce.1 = f32[32]{0:T(128)S(1)} all-reduce(f32[32]{0:T(128)S(1)} %reshape.100), channel_id=1, replica_groups=mesh['ctx'=4,'head'=4,'fsdp'=2] {'head','fsdp'}, use_global_device_ids=true, to_apply=%add | all-reduce | flops 32 | bytes 256
  148.4 0.1 fusion.76
  148.5 0.1 broadcast_bitcast_fusion
  148.6 0.1 broadcast_in_dim.65
  148.7 0.1 broadcast_in_dim.66
  148.7 0.1 mul.102
  148.8 0.0 copy-done.8
  148.9 4.8 %fusion.49 = f32[512,4,128]{0,2,1:T(8,128)S(1)} fusion(bf16[1024,4,128]{0,2,1:T(8,128)(2,1)S(1)} %copy-done.8, f32[4,512,1024]{2,1,0:T(8,128)} %copy-done.4, f32[4,512]{1,0:T(4,128)S(1)} %is-finite_select_fusion.7, pred[512,1024]{1,0:T(8,128)(4,1)S(1)} %copy-done.6, f32[512,4]{0,1:T(4,128)S(1)} %get-tuple-element.15), kind=kOutput, calls=%fused_computation.41 | convolution fusion | flops 545521664 | bytes 11026432 | tf_op jit(solution)/shard_map/htu,uhd->thd/dot_general | solution.py:26
  153.7 0.0 collective-permute-done.1
  153.7 1.0 copy-done.2
  154.7 3.5 %divide_convert_fusion.1 = bf16[512,4,128]{0,2,1:T(8,128)(2,1)S(1)} fusion(f32[512,4,128]{0,2,1:T(8,128)S(1)} %fusion.49, bf16[1024,4,128]{0,2,1:T(8,128)(2,1)} %bitcast.15, f32[4,512,1024]{2,1,0:T(8,128)S(1)} %copy-done.2, f32[4,512]{1,0:T(4,128)S(1)} %is-finite_select_fusion.4, pred[]{:T(512)S(6)} %gt.4, f32[512,4]{0,1:T(4,128)S(1)} %get-tuple-element.13, ...), kind=kOutput, calls=%fused_computation.48 | convolution fusion | flops 546308096 | bytes 11034625 | tf_op jit(solution)/shard_map/htu,uhd->thd/dot_general | solution.py:26
  158.2 0.2 copy.34
  158.4 4.7 %fusion.46 = f32[512,4,128]{0,2,1:T(8,128)S(1)} fusion(bf16[1024,4,128]{0,2,1:T(8,128)(2,1)S(1)} %copy-done.8, f32[4,512,1024]{2,1,0:T(8,128)} %copy-done.3, f32[4,512]{1,0:T(4,128)S(1)} %is-finite_select_fusion.3, pred[512,1024]{1,0:T(8,128)(4,1)S(1)} %copy-done.5, f32[512,4]{0,1:T(4,128)S(1)} %get-tuple-element.18), kind=kOutput, calls=%fused_computation.40 | convolution fusion | flops 545521664 | bytes 11026432 | tf_op jit(solution)/shard_map/htu,uhd->thd/dot_general | solution.py:26
  163.1 0.0 copy-start.13
  163.1 0.0 copy-start.14
  163.1 5.8 %divide_convert_fusion = bf16[512,4,128]{0,2,1:T(8,128)(2,1)S(1)} fusion(f32[512,4,128]{0,2,1:T(8,128)S(1)} %fusion.46, bf16[1024,4,128]{0,2,1:T(8,128)(2,1)} %bitcast.15, f32[4,512,1024]{2,1,0:T(8,128)} %copy-done, f32[4,512]{1,0:T(4,128)S(1)} %is-finite_select_fusion, pred[]{:T(512)S(6)} %gt.4, f32[512,4]{0,1:T(4,128)S(1)} %get-tuple-element.16, ...), kind=kOutput, calls=%fused_computation.47 | convolution fusion | flops 546308096 | bytes 11034625 | tf_op jit(solution)/shard_map/htu,uhd->thd/dot_general | solution.py:26
  169.0 0.2 copy.35
  169.2 0.9 multiply_convert_fusion
  170.1 0.7 multiply_convert_fusion.1
  170.8 1.0 pad_maximum_fusion.1
  (33 shorter events, 0.1 us)
Async XLA Ops:
  1.9 46.6 %copy-start.15 = (u32[32]{0:T(128)S(1)}, u32[32]{0:T(128)}, u32[]{:S(2)}) copy-start(u32[32]{0:T(128)} %constant.30) | copy-start | bytes 388
  3.0 18.8 %all-to-all-start = ((bf16[4,256,512]{2,1,0:T(8,128)(2,1)}), bf16[4,256,512]{2,1,0:T(8,128)(2,1)S(1)}, u32[]{:S(2)}, u32[]{:S(2)}) async-start(bf16[4,256,512]{2,1,0:T(8,128)(2,1)} %pad_maximum_fusion), calls=%async_computation | async-start | bytes 2097152 | tf_op jit(solution)/shard_map/all_to_all | solution.py:61
  21.8 22.3 %all-to-all-start.2 = ((bf16[256,4,768]{0,2,1:T(8,128)(2,1)}), bf16[256,4,768]{0,2,1:T(8,128)(2,1)S(1)}, u32[]{:S(2)}, u32[]{:S(2)}) async-start(bf16[256,4,768]{0,2,1:T(8,128)(2,1)} %bitcast.117), calls=%async_computation.2 | async-start | bytes 3145728 | tf_op jit(solution)/shard_map/all_to_all | solution.py:59
  44.1 23.2 %all-to-all-start.1 = ((bf16[256,4,768]{0,2,1:T(8,128)(2,1)}), bf16[256,4,768]{0,2,1:T(8,128)(2,1)}, u32[]{:S(2)}, u32[]{:S(2)}) async-start(bf16[256,4,768]{0,2,1:T(8,128)(2,1)} %bitcast.116), calls=%async_computation.1 | async-start | bytes 3145728 | tf_op jit(solution)/shard_map/all_to_all | solution.py:58
  58.3 36.7 %collective-permute-start = (bf16[1024,768]{1,0:T(8,128)(2,1)}, bf16[1024,768]{1,0:T(8,128)(2,1)}, u32[]{:S(2)}, u32[]{:S(2)}) collective-permute-start(bf16[1024,768]{1,0:T(8,128)(2,1)} %bitcast.11), channel_id=1, source_target_pairs={{0,8},{8,16},{16,24},{1,9},{9,17},{17,25},{2,10},{10,18},{18,26},{... | collective-permute-start | bytes 4718600 | tf_op jit(solution)/shard_map/ppermute | solution.py:16
  74.4 6.3 %copy-start.6 = (pred[512,1024]{1,0:T(8,128)(4,1)S(1)}, pred[512,1024]{1,0:T(8,128)(4,1)}, u32[]{:S(2)}) copy-start(pred[512,1024]{1,0:T(8,128)(4,1)} %iota_compare_fusion.1) | copy-start | bytes 1572868
  76.9 3.8 %copy-start.7 = (bf16[1024,4,192]{0,2,1:T(8,128)(2,1)S(1)}, bf16[1024,4,192]{0,2,1:T(8,128)(2,1)}, u32[]{:S(2)}) copy-start(bf16[1024,4,192]{0,2,1:T(8,128)(2,1)} %reshape.95) | copy-start | bytes 4718596
  76.9 3.8 %copy-start.11 = (bf16[512,4,192]{0,2,1:T(8,128)(2,1)S(1)}, bf16[512,4,192]{0,2,1:T(8,128)(2,1)}, u32[]{:S(2)}) copy-start(bf16[512,4,192]{0,2,1:T(8,128)(2,1)} %slice.15) | copy-start | bytes 2359300
  80.8 7.6 %copy-start.3 = (f32[4,512,1024]{2,1,0:T(8,128)}, f32[4,512,1024]{2,1,0:T(8,128)S(1)}, u32[]{:S(2)}) copy-start(f32[4,512,1024]{2,1,0:T(8,128)S(1)} %get-tuple-element.26) | copy-start | bytes 25165828
  80.8 2.0 %copy-start.5 = (pred[512,1024]{1,0:T(8,128)(4,1)S(1)}, pred[512,1024]{1,0:T(8,128)(4,1)}, u32[]{:S(2)}) copy-start(pred[512,1024]{1,0:T(8,128)(4,1)} %iota_compare_fusion) | copy-start | bytes 1572868
  82.7 5.7 %copy-start.4 = (f32[4,512,1024]{2,1,0:T(8,128)}, f32[4,512,1024]{2,1,0:T(8,128)S(1)}, u32[]{:S(2)}) copy-start(f32[4,512,1024]{2,1,0:T(8,128)S(1)} %get-tuple-element.30) | copy-start | bytes 25165828
  82.8 14.0 %copy-start.10 = (bf16[512,4,192]{0,2,1:T(8,128)(2,1)S(1)}, bf16[512,4,192]{0,2,1:T(8,128)(2,1)}, u32[]{:S(2)}) copy-start(bf16[512,4,192]{0,2,1:T(8,128)(2,1)} %slice.17) | copy-start | bytes 2359300
  96.7 1.5 copy-start.12
  98.3 6.1 %copy-start = (f32[4,512,1024]{2,1,0:T(8,128)}, f32[4,512,1024]{2,1,0:T(8,128)S(1)}, u32[]{:S(2)}) copy-start(f32[4,512,1024]{2,1,0:T(8,128)S(1)} %get-tuple-element.28) | copy-start | bytes 25165828
  99.8 4.6 %copy-start.1 = (f32[4,512,1024]{2,1,0:T(8,128)}, f32[4,512,1024]{2,1,0:T(8,128)S(1)}, u32[]{:S(2)}) copy-start(f32[4,512,1024]{2,1,0:T(8,128)S(1)} %get-tuple-element.32) | copy-start | bytes 25165828
  99.8 4.6 %copy-start.9 = (bf16[1024,512]{0,1:T(8,128)(2,1)S(1)}, bf16[1024,512]{0,1:T(8,128)(2,1)}, u32[]{:S(2)}) copy-start(bf16[1024,512]{0,1:T(8,128)(2,1)} %copy.32) | copy-start | bytes 3145732
  99.8 49.0 %copy-start.8 = (bf16[1024,4,128]{0,2,1:T(8,128)(2,1)S(1)}, bf16[1024,4,128]{0,2,1:T(8,128)(2,1)}, u32[]{:S(2)}) copy-start(bf16[1024,4,128]{0,2,1:T(8,128)(2,1)} %copy.37) | copy-start | bytes 3145732
  104.5 49.2 %collective-permute-start.1 = (bf16[1024,512]{0,1:T(8,128)(2,1)S(1)}, bf16[1024,512]{0,1:T(8,128)(2,1)}, u32[]{:S(2)}, u32[]{:S(2)}) collective-permute-start(bf16[1024,512]{0,1:T(8,128)(2,1)S(1)} %copy-done.9), channel_id=1, source_target_pairs={{0,8},{8,16},{16,24},{1,9},{9,17},{17,25},{2,10},{10,18},{18,26},{... | collective-permute-start | bytes 3145736 | tf_op jit(solution)/shard_map/ppermute | solution.py:16
  148.8 5.8 %copy-start.2 = (f32[4,512,1024]{2,1,0:T(8,128)S(1)}, f32[4,512,1024]{2,1,0:T(8,128)}, u32[]{:S(2)}) copy-start(f32[4,512,1024]{2,1,0:T(8,128)} %copy-done.1) | copy-start | bytes 25165828
  163.1 6.1 %copy-start.13 = (bf16[192,1536]{1,0:T(8,128)(2,1)S(1)}, bf16[192,1536]{1,0:T(8,128)(2,1)}, u32[]{:S(2)}) copy-start(bf16[192,1536]{1,0:T(8,128)(2,1)} %param.8) | copy-start | bytes 1769476
  163.1 7.0 %copy-start.14 = (bf16[64,1024]{1,0:T(8,128)(2,1)S(1)}, bf16[64,1024]{1,0:T(8,128)(2,1)}, u32[]{:S(2)}) copy-start(bf16[64,1024]{1,0:T(8,128)(2,1)} %param.9) | copy-start | bytes 393220
